TPU v7x, 32 devices: a whole 2x2x4 slice. The times are simulated.
32 devices in a mesh: groups: 2 (over y), row: 4 (over x, core), col: 4 (over z).
Axes of the slice: x: 2, y: 2, z: 4, core: 2. Of those that a mesh axis runs over, the one named last changes fastest.
Arguments:
- right_sides: float32 [32, 16384], P(None, ('groups', 'row')), parts along dimension 1
- nugget: float32 [16384], P(('groups', 'row')), parts along dimension 0, may hold values from 1 to 4
- cov_blocks: bfloat16 [8, 4, 32, 256, 256], P(('groups', 'row'), 'col'), parts along dimension 0
- block_rows: int32 [8, 4, 32], P(('groups', 'row'), 'col'), parts along dimension 0, may hold values from 0 to 7, as said below
- block_cols: int32 [8, 4, 32], P(('groups', 'row'), 'col'), parts along dimension 0, may hold values from 0 to 7, as said below
- block_count: int32 [8, 4], P(('groups', 'row'), 'col'), parts along dimension 0, may hold values from 4 to 32, as said below
Outputs:
- solution: float32 [32, 16384], P(None, ('groups', 'row')), parts along dimension 1
- residual: float32 [32, 16384], P(None, ('groups', 'row')), parts along dimension 1
There are 2 independent parts, one for each index of `groups`. A program takes and returns all parts, laid end to end along the dimension named above; each array names one. Nothing has to cross between parts.
Inputs may be any that keep to these rules, and one draw needn't show every extreme that they name: On each device the pairs (block_rows, block_cols) of all 32 slots are distinct; no stored block position of a problem is the mirror image of another (no pair is stored both as (g, h) and as (h, g)); on devices whose row and col index are equal, block_rows <= block_cols. `block_cols`: see block_rows. `block_count`: slots at or beyond the count are empty; some device of every problem has exactly 32 live slots.
All inputs are finite; a program needn't handle non-finite values.
Results may differ from a plain program's by a relative error of at most 0.0003.
Values sent between devices are 32-bit elements; how exact they have to be, the bound alone decides.
A program may use at most 64 MiB of HBM per device.

v0:
```python
import jax
import jax.numpy as jnp
from jax import lax
from jax.sharding import PartitionSpec as P

ITERS = 2


def from_root(value, axis, source):
    kept = jnp.where(lax.axis_index(axis) == source, value, 0).astype(value.dtype)
    return lax.psum(kept, axis)


def on_device(right_sides, nugget, cov_blocks, block_rows, block_cols, block_count):
    blocks = cov_blocks[0, 0].astype(jnp.float32)
    slot_rows = block_rows[0, 0]
    slot_cols = block_cols[0, 0]
    live_count = block_count[0, 0]
    slot_total = blocks.shape[0]
    tile_size = blocks.shape[1]
    series, row_width = right_sides.shape
    tile_count = row_width // tile_size
    live_mask = (jnp.arange(slot_total, dtype=jnp.int32) < live_count).astype(jnp.float32)
    block_ids = jnp.arange(tile_count, dtype=jnp.int32)[:, None]
    row_selector = (slot_rows[None, :] == block_ids).astype(jnp.float32) * live_mask[None, :]
    col_selector = (slot_cols[None, :] == block_ids).astype(jnp.float32) * live_mask[None, :]

    def spread(selector, values):
        placed = jnp.einsum("bm,rmj->rbj", selector, values, precision=lax.Precision.HIGHEST)
        return placed.reshape(series, row_width)

    solution = jnp.zeros_like(right_sides)
    residual = right_sides
    direction = right_sides
    norm_now = lax.psum(jnp.sum(residual * residual, axis=1), "row")
    for turn_index in range(ITERS):
        far_rows = from_root(direction, "row", lax.axis_index("col"))
        near_tiles = direction.reshape(series, tile_count, tile_size)
        far_tiles = far_rows.reshape(series, tile_count, tile_size)
        local_direct = jnp.einsum(
            "rmk,mjk->rmj",
            jnp.take(far_tiles, slot_cols, axis=1),
            blocks,
            precision=lax.Precision.HIGHEST,
        )
        local_mirror = jnp.einsum(
            "rmj,mjk->rmk",
            jnp.take(near_tiles, slot_rows, axis=1),
            blocks,
            precision=lax.Precision.HIGHEST,
        )
        apply_direct = spread(row_selector, local_direct)
        apply_mirror = spread(col_selector, local_mirror)
        total = lax.psum(apply_direct, "col")
        summed = lax.psum(apply_mirror, "row")
        total = total + from_root(summed, "col", lax.axis_index("row"))
        applied = nugget[None, :] * direction + total
        curvature, crossed, squared = lax.psum(
            (
                jnp.sum(direction * applied, axis=1),
                jnp.sum(residual * applied, axis=1),
                jnp.sum(applied * applied, axis=1),
            ),
            "row",
        )
        step_size = norm_now / curvature
        solution = solution + step_size[:, None] * direction
        residual = residual - step_size[:, None] * applied
        norm_next = norm_now - 2.0 * step_size * crossed + step_size * step_size * squared
        direction = residual + (norm_next / norm_now)[:, None] * direction
        norm_now = norm_next
    return (solution, residual)


def solution(mesh):
    placed = (
        P(None, ("groups", "row")),
        P(("groups", "row")),
        P(("groups", "row"), "col", None, None, None),
        P(("groups", "row"), "col", None),
        P(("groups", "row"), "col", None),
        P(("groups", "row"), "col"),
    )
    return jax.shard_map(
        on_device,
        mesh=mesh,
        in_specs=placed,
        out_specs=(P(None, ("groups", "row")), P(None, ("groups", "row"))),
        check_vma=False,
    )
```

profile of v0, /device:TPU:0, one launch (start us, length us, event | category | flops | bytes accessed | tf_op | source)
XLA Modules:
  0.0 210.6 jit_solution(2557300919919235164)
XLA Ops:
  7.2 0.0 all-reduce.14.cloned.1.call-start
  7.2 0.7 compare_and_fusion
  7.9 0.7 compare_select_fusion
  9.2 1.0 copy.38
  10.2 1.0 broadcast_select_fusion.1
  11.2 0.7 copy.39
  11.9 0.6 gather_fusion.1
  12.5 4.4 %fusion.11 = f32[32,32,256]{2,0,1:T(8,128)S(1)} fusion(bf16[1,1,32,256,256]{4,3,2,1,0:T(8,128)(2,1)} %param.10, f32[32,32,256]{2,1,0:T(8,128)S(1)} %gather_fusion.1, pred[32]{0:T(512)(128)(4,1)S(1)} %compare_and_fusion), kind=kOutput, calls=%fused_computation.13 | convolution fusion | flops 805568512 | bytes 6291488 | tf_op jit(solution)/shard_map/rmj,mjk->rmk/dot_general | solution.py:46
  16.9 0.0 copy-done.5
  16.9 1.2 fusion.28
  18.2 0.8 copy.21
  18.9 0.0 all-reduce.14.cloned.1.call-update
  19.0 0.0 all-reduce.8.cloned.1.call-start
  19.1 35.7 %all-reduce.14.cloned.1.call-done = (f32[32,8,256]{2,0,1:T(8,128)}, f32[32,2048]{1,0:T(8,128)}) async-done(((f32[32,8,256]{2,0,1:T(8,128)}, f32[32,2048]{1,0:T(8,128)}), (f32[32,8,256]{2,0,1:T(8,128)}, f32[32,2048]{1,0:T(8,128)})) %all-reduce.14.cloned.1.call-update) | async-done | bytes 524304 | tf_op jit(solution)/shard_map/psum | solution.py:11
  54.8 1.6 gather_fusion
  56.4 0.0 copy-start.2
  56.4 0.0 copy-start
  56.4 0.0 copy-start.4
  56.4 6.0 %fusion.8 = f32[32,32,256]{2,0,1:T(8,128)S(1)} fusion(bf16[1,1,32,256,256]{4,3,2,1,0:T(8,128)(2,1)} %param.10, f32[32,32,256]{2,1,0:T(8,128)S(1)} %gather_fusion, pred[32]{0:T(512)(128)(4,1)S(1)} %compare_and_fusion.1), kind=kOutput, calls=%fused_computation.12 | convolution fusion | flops 805568512 | bytes 6291488 | tf_op jit(solution)/shard_map/rmk,mjk->rmj/dot_general | solution.py:40
  62.4 0.0 copy-done.6
  62.4 1.2 fusion.30
  63.7 0.1 copy.20
  63.8 0.7 select_add_fusion.1
  64.5 0.0 all-reduce.8.cloned.1.call-update
  64.5 0.0 all-reduce.12.cloned.1.call-start
  64.6 35.8 %all-reduce.8.cloned.1.call-done = f32[32,2048]{1,0:T(8,128)} async-done(((f32[32,2048]{1,0:T(8,128)}), f32[32,2048]{1,0:T(8,128)}) %all-reduce.8.cloned.1.call-update) | async-done | bytes 262160 | tf_op jit(solution)/shard_map/psum | solution.py:54
  100.4 1.2 multiply_reduce_fusion.2
  101.6 5.7 %all-reduce = (f32[32]{0:T(128)S(1)}, f32[32]{0:T(128)S(1)}, f32[32]{0:T(128)S(1)}) all-reduce(f32[32]{0:T(128)S(1)} %get-tuple-element.4, f32[32]{0:T(128)S(1)} %get-tuple-element.5, f32[32]{0:T(128)S(1)} %get-tuple-element.3), channel_id=1, replica_groups=mesh['groups'=2,'row'=4,'col'=4] {'row'}, use_global_device_ids=true, to_apply=%region_9.11 | all-reduce | flops 96 | bytes 768 | tf_op jit(solution)/shard_map/psum | solution.py:58
  107.3 1.1 broadcast_select_fusion
  108.3 0.7 copy.37
  109.1 0.6 gather_fusion.3
  109.7 4.4 %fusion.17 = f32[32,32,256]{2,0,1:T(8,128)S(1)} fusion(bf16[1,1,32,256,256]{4,3,2,1,0:T(8,128)(2,1)} %param.10, f32[32,32,256]{2,1,0:T(8,128)S(1)} %gather_fusion.3, pred[32]{0:T(512)(128)(4,1)S(1)} %compare_and_fusion), kind=kOutput, calls=%fused_computation.15 | convolution fusion | flops 805568512 | bytes 6291488 | tf_op jit(solution)/shard_map/rmj,mjk->rmk/dot_general | solution.py:46
  114.1 1.2 fusion.24
  115.3 0.8 copy.23
  116.1 0.0 all-reduce.12.cloned.1.call-update
  116.1 0.2 all-reduce.10.cloned.1.call-start
  116.4 33.5 %all-reduce.12.cloned.1.call-done = (f32[32,8,256]{2,0,1:T(8,128)}, f32[32,2048]{1,0:T(8,128)}) async-done(((f32[32,8,256]{2,0,1:T(8,128)}, f32[32,2048]{1,0:T(8,128)}), (f32[32,8,256]{2,0,1:T(8,128)}, f32[32,2048]{1,0:T(8,128)})) %all-reduce.12.cloned.1.call-update) | async-done | bytes 524304 | tf_op jit(solution)/shard_map/psum | solution.py:11
  149.9 1.6 gather_fusion.2
  151.5 6.0 %fusion.14 = f32[32,32,256]{2,0,1:T(8,128)S(1)} fusion(bf16[1,1,32,256,256]{4,3,2,1,0:T(8,128)(2,1)} %param.10, f32[32,32,256]{2,1,0:T(8,128)S(1)} %gather_fusion.2, pred[32]{0:T(512)(128)(4,1)S(1)} %compare_and_fusion.1), kind=kOutput, calls=%fused_computation.14 | convolution fusion | flops 805568512 | bytes 6291488 | tf_op jit(solution)/shard_map/rmk,mjk->rmj/dot_general | solution.py:40
  157.5 1.2 fusion.26
  158.7 0.1 copy.22
  158.8 0.7 select_add_fusion
  159.6 0.0 all-reduce.10.cloned.1.call-update
  159.6 35.9 %all-reduce.10.cloned.1.call-done = f32[32,2048]{1,0:T(8,128)} async-done(((f32[32,2048]{1,0:T(8,128)}), f32[32,2048]{1,0:T(8,128)}) %all-reduce.10.cloned.1.call-update) | async-done | bytes 262160 | tf_op jit(solution)/shard_map/psum | solution.py:54
  195.4 1.1 multiply_reduce_fusion
  196.5 5.7 %psum.98 = f32[32]{0:T(128)S(1)} all-reduce(f32[32]{0:T(128)S(1)} %multiply_reduce_fusion), channel_id=1, replica_groups=mesh['groups'=2,'row'=4,'col'=4] {'row'}, use_global_device_ids=true, to_apply=%region_15.17 | all-reduce | flops 32 | bytes 256 | tf_op jit(solution)/shard_map/psum | solution.py:58
  202.2 0.0 copy-done.1
  202.2 1.9 multiply_subtract_fusion
  (16 shorter events, 0.1 us)
Async XLA Ops:
  7.2 47.6 %all-reduce.14.cloned.1.call-start = ((), (), s32[]{:S(2)}) async-start(), calls=%async_computation.3 | async-start | bytes 1048576 | tf_op jit(solution)/shard_map/psum | solution.py:11
  11.9 5.0 %copy-start.5 = (s32[1,1,32]{2,1,0:T(1,128)S(1)}, s32[1,1,32]{2,1,0:T(1,128)}, u32[]{:S(2)}) copy-start(s32[1,1,32]{2,1,0:T(1,128)} %param.12) | copy-start | bytes 388
  19.0 81.4 %all-reduce.8.cloned.1.call-start = ((), (), s32[]{:S(2)}) async-start(), calls=%async_computation | async-start | bytes 524288 | tf_op jit(solution)/shard_map/psum | solution.py:54
  54.8 7.6 %copy-start.6 = (s32[1,1,32]{2,1,0:T(1,128)S(1)}, s32[1,1,32]{2,1,0:T(1,128)}, u32[]{:S(2)}) copy-start(s32[1,1,32]{2,1,0:T(1,128)} %param.11) | copy-start | bytes 388
  56.4 7.4 %copy-start.2 = (f32[32,2048]{1,0:T(8,128)S(1)}, f32[32,2048]{1,0:T(8,128)}, u32[]{:S(2)}) copy-start(f32[32,2048]{1,0:T(8,128)} %get-tuple-element.12) | copy-start | bytes 786436
  56.4 44.0 %copy-start = (f32[32,2048]{1,0:T(8,128)S(1)}, f32[32,2048]{1,0:T(8,128)}, u32[]{:S(2)}) copy-start(f32[32,2048]{1,0:T(8,128)} %param.8) | copy-start | bytes 786436
  56.4 44.0 %copy-start.4 = (f32[2048]{0:T(1024)S(1)}, f32[2048]{0:T(1024)}, u32[]{:S(2)}) copy-start(f32[2048]{0:T(1024)} %param.9) | copy-start | bytes 24580
  64.5 85.4 %all-reduce.12.cloned.1.call-start = ((), (), s32[]{:S(2)}) async-start(), calls=%async_computation.2 | async-start | bytes 1048576 | tf_op jit(solution)/shard_map/psum | solution.py:11
  116.1 79.3 %all-reduce.10.cloned.1.call-start = ((), (), s32[]{:S(2)}) async-start(), calls=%async_computation.1 | async-start | bytes 524288 | tf_op jit(solution)/shard_map/psum | solution.py:54
  151.5 7.4 %copy-start.3 = (f32[32,2048]{1,0:T(8,128)S(1)}, f32[32,2048]{1,0:T(8,128)}, u32[]{:S(2)}) copy-start(f32[32,2048]{1,0:T(8,128)} %get-tuple-element.10) | copy-start | bytes 786436
  151.5 50.7 %copy-start.1 = (f32[32,2048]{1,0:T(8,128)S(1)}, f32[32,2048]{1,0:T(8,128)}, u32[]{:S(2)}) copy-start(f32[32,2048]{1,0:T(8,128)} %all-reduce.8.cloned.1.call-done) | copy-start | bytes 786436
Sparse Core Ops, SparseCore 0:
  19.1 35.6 all-reduce.13
  64.6 35.7 all-reduce.7
  116.3 33.5 all-reduce.11
  159.7 35.6 all-reduce.9
where the time goes:
time: 211 us
  waiting for transfers between devices  141 us (67%)
  matrix products  25.7 us (12%)
  between operations  14.7 us (7%)
  blocking collectives  11.3 us (5%)
  other arithmetic  9.03 us (4%)
  local copies, waits for them, and re-layouts  8.58 us (4%)
    psum x2, waiting for transfers between devices, on_device(): total = lax.psum(apply_direct, 'col')  71.7 us
    psum x2, waiting for transfers between devices, from_root(): return lax.psum(kept, axis)  69.2 us
    dot_general x2, matrix products, on_device(): jnp.einsum('rmk,mjk->rmj', jnp.take(far_tiles, slot_cols, axis=1), blocks...  12 us
    psum x2, blocking collectives, on_device(): lax.psum((jnp.sum(direction * applied, axis=1), jnp.sum(residual * applie...  11.3 us
    dot_general x2, matrix products, on_device(): jnp.einsum('rmj,mjk->rmk', jnp.take(near_tiles, slot_rows, axis=1), block...  8.74 us
    dot_general x4, matrix products, spread(): jnp.einsum('bm,rmj->rbj', selector, values, precision=lax.Precision.HIGHEST)  4.95 us
  transfers between devices with their start and end apart: 4, of which 4 were waited for; matrix products, arithmetic and copies ran while one was open for 0% of the time, Pallas kernels for 0%

commit v1 on v0

v1 whole, which is shorter than its diff:
```python
import functools

import jax
import jax.numpy as jnp
from jax import lax
from jax.experimental import pallas as pl
from jax.experimental.pallas import tpu as pltpu
from jax.sharding import PartitionSpec as P

ITERS = 2
LANES = 128
CORES = 2
PIECES = 3
UNROLL = 8


def kernel(
    n_row, n_col,
    cols_ref, rows_ref, pos_ref, rhs_ref, nugget_ref, stored_ref,
    solution_ref, residual_ref,
    blocks, vec, far, near_x, far_x, products, direct, mirror,
    m_part, m_half, m_root, rs_in, r_one, p_one, ex_out, ex_in,
    block_sem, far_send, far_recv, fwd_send, mp_send, mp_recv, mr_send, mr_recv,
    rs_send, rs_recv, ag_send, ag_recv, ex_send, ex_recv,
):
    groups, series, _ = vec.shape[1:]
    slots, tile, _ = blocks.shape
    tiles = near_x.shape[0]
    per_tile = tile // LANES
    chunk = groups // n_col
    chips = n_row // CORES
    half_rows = series // CORES
    me_row = lax.axis_index("row")
    me_col = lax.axis_index("col")
    chip, core = me_row // CORES, lax.rem(me_row, CORES)
    partner = chip * CORES + (1 - core)
    root = me_col
    root_chip = root // CORES
    is_root = me_row == root
    on_root_chip = chip == root_chip
    is_root_partner = jnp.logical_and(on_root_chip, jnp.logical_not(is_root))
    away = jnp.logical_not(on_root_chip)
    finals = []

    def copy(src, dst, send_sem, recv_sem, **where):
        return pltpu.make_async_remote_copy(
            src_ref=src, dst_ref=dst, send_sem=send_sem, recv_sem=recv_sem,
            device_id=where, device_id_type=pl.DeviceIdType.MESH)

    def arrived(dst, recv_sem, send_sem):
        copy(dst, dst, send_sem, recv_sem, row=partner).wait_recv()

    def own_half(ref, which):
        return ref.at[:, pl.ds(pl.multiple_of(which * half_rows, half_rows), half_rows), :]

    def part(k):
        return pl.ds(k * chunk, chunk)

    barrier = pltpu.get_barrier_semaphore()
    for j in range(1, n_row):
        pl.semaphore_signal(barrier, inc=1, device_id={"row": lax.rem(me_row + j, n_row)},
                            device_id_type=pl.DeviceIdType.MESH)
    for j in range(1, n_col):
        pl.semaphore_signal(barrier, inc=1, device_id={"col": lax.rem(me_col + j, n_col)},
                            device_id_type=pl.DeviceIdType.MESH)
    fetch = pltpu.make_async_copy(stored_ref, blocks, block_sem)
    fetch.start()

    def split_into(dst, src):
        def one(t, carry):
            whole = jnp.concatenate([src[t * per_tile + k] for k in range(per_tile)], axis=1)
            rest = whole
            for piece in range(PIECES):
                top = rest.astype(jnp.bfloat16)
                dst[t, piece * series:(piece + 1) * series, :] = top
                rest = rest - top.astype(jnp.float32)
            return carry
        lax.fori_loop(0, tiles, one, 0)

    def multiply(pick_ref, x_ref, contract):
        def some(step, carry):
            for k in range(UNROLL):
                s = step * UNROLL + k
                out = lax.dot_general(x_ref[pick_ref[s]], blocks[s],
                                      (((1,), (contract,)), ((), ())),
                                      preferred_element_type=jnp.float32)
                total = out[(PIECES - 1) * series:]
                for piece in range(PIECES - 2, -1, -1):
                    total = total + out[piece * series:(piece + 1) * series]
                products[s] = total
            return carry
        lax.fori_loop(0, slots // UNROLL, some, 0)

    def collect(dst, by_row):
        def one(t, carry):
            total = None
            for k in range(tiles):
                term = products[pos_ref[t * tiles + k] if by_row else pos_ref[k * tiles + t]]
                total = term if total is None else total + term
            for k in range(per_tile):
                dst[t * per_tile + k] = total[:, k * LANES:(k + 1) * LANES]
            return carry
        lax.fori_loop(0, tiles, one, 0)

    def dot(left, right):
        def one(g, total):
            return total + left(g) * right(g)
        return lax.fori_loop(0, groups, one, jnp.zeros((series, LANES), jnp.float32), unroll=4)

    def exchange_start(k, parts):
        for q, value in enumerate(parts):
            ex_out[k, q] = value
        count = len(parts)
        for j in range(1, n_row):
            c = copy(ex_out.at[k, pl.ds(0, count)], ex_in.at[k, j - 1, pl.ds(0, count)],
                     ex_send.at[k, j - 1], ex_recv.at[k, j - 1],
                     row=lax.rem(me_row + j, n_row))
            c.start()
            finals.append(c.wait_send)

    def exchange_done(k, count):
        for j in range(1, n_row):
            arrived(ex_in.at[k, j - 1, pl.ds(0, count)], ex_recv.at[k, j - 1], ex_send.at[k, j - 1])
        sums = []
        for q in range(count):
            total = ex_out[k, q]
            for j in range(1, n_row):
                total = total + ex_in[k, j - 1, q]
            sums.append(jnp.sum(total, axis=1, keepdims=True))
        return sums

    def far_start(i):
        for j in range(1, chips):
            for h in range(CORES):
                c = copy(own_half(vec.at[i], h), own_half(far.at[i], h),
                         far_send.at[i, j, h], far_recv.at[i, h],
                         row=lax.rem(root_chip + j, chips) * CORES + h)
                pl.when(is_root)(c.start)
                finals.append(lambda c=c: pl.when(is_root)(c.wait_send))
        for h in range(CORES):
            c = copy(own_half(vec.at[i], h), own_half(far.at[i], h),
                     far_send.at[i, 0, h], far_recv.at[i, h], row=partner)
            pl.when(is_root)(c.start)
            finals.append(lambda c=c: pl.when(is_root)(c.wait_send))

    def far_relay(i):
        def go():
            mine = own_half(far.at[i], core)
            arrived(mine, far_recv.at[i, core], fwd_send.at[i])
            copy(mine, mine, fwd_send.at[i], far_recv.at[i, core], row=partner).start()
        pl.when(away)(go)
        mine = own_half(far.at[i], core)
        c = copy(mine, mine, fwd_send.at[i], far_recv.at[i, core], row=partner)
        finals.append(lambda: pl.when(away)(c.wait_send))

    def far_done(i):
        def last():
            arrived(own_half(far.at[i], 1 - core), far_recv.at[i, 1 - core], fwd_send.at[i])
        def both():
            for h in range(CORES):
                arrived(own_half(far.at[i], h), far_recv.at[i, h], fwd_send.at[i])
        pl.when(away)(last)
        pl.when(is_root_partner)(both)
        pl.when(is_root)(lambda: split_into(far_x, vec.at[i]))
        pl.when(jnp.logical_not(is_root))(lambda: split_into(far_x, far.at[i]))

    def mirror_start(i):
        other = copy(own_half(mirror.at[i], 1 - core), m_part.at[i], mp_send.at[i], mp_recv.at[i], row=partner)
        whole = copy(mirror.at[i], m_root.at[i, chips - 1], mp_send.at[i],
                     mr_recv.at[i, chips - 1, 0], row=root)
        pl.when(away)(other.start)
        pl.when(is_root_partner)(whole.start)
        finals.append(lambda: pl.when(away)(other.wait_send))
        finals.append(lambda: pl.when(is_root_partner)(whole.wait_send))

    def mirror_relay(i):
        slot = lax.rem(chip - root_chip + chips, chips) - 1
        slot = jnp.maximum(slot, 0)
        onward = copy(m_half.at[i], own_half(m_root.at[i, slot], core), mr_send.at[i],
                      mr_recv.at[i, slot, core], row=root)
        def go():
            arrived(m_part.at[i], mp_recv.at[i], mp_send.at[i])
            first = pl.multiple_of(core * half_rows, half_rows)
            def one(g, carry):
                m_half[i, g] = mirror[i, g, pl.ds(first, half_rows), :] + m_part[i, g]
                return carry
            lax.fori_loop(0, groups, one, 0, unroll=4)
            onward.start()
        pl.when(away)(go)
        finals.append(lambda: pl.when(away)(onward.wait_send))

    def mirror_done(i):
        def go():
            for j in range(chips - 1):
                for h in range(CORES):
                    arrived(own_half(m_root.at[i, j], h), mr_recv.at[i, j, h], mr_send.at[i])
            arrived(m_root.at[i, chips - 1], mr_recv.at[i, chips - 1, 0], mr_send.at[i])
            def one(g, carry):
                total = direct[i, g] + mirror[i, g]
                for j in range(chips):
                    total = total + m_root[i, j, g]
                direct[i, g] = total
                return carry
            lax.fori_loop(0, groups, one, 0, unroll=2)
        pl.when(is_root)(go)

    def reduce_start(i):
        for j in range(n_col - 1, 0, -1):
            to = lax.rem(me_col + j, n_col)
            c = copy(direct.at[i, part(to)], rs_in.at[i, j - 1], rs_send.at[i, j - 1],
                     rs_recv.at[i, j - 1], col=to)
            c.start()
            finals.append(c.wait_send)

    def reduce_done(i):
        for j in range(1, n_col):
            arrived(rs_in.at[i, j - 1], rs_recv.at[i, j - 1], rs_send.at[i, j - 1])
        for k in range(chunk):
            g = me_col * chunk + k
            total = direct[i, g] + nugget_ref[pl.ds(g, 1), :] * vec[i, g]
            for j in range(1, n_col):
                total = total + rs_in[i, j - 1, k]
            vec[i + 1, g] = total

    def gather_start(i):
        mine = vec.at[i + 1, part(me_col)]
        for j in range(n_col - 1, 0, -1):
            c = copy(mine, mine, ag_send.at[i, j - 1], ag_recv.at[i, j - 1],
                     col=lax.rem(me_col + j, n_col))
            c.start()
            finals.append(c.wait_send)

    def gather_done(i):
        for j in range(1, n_col):
            arrived(vec.at[i + 1, part(lax.rem(me_col - j + n_col, n_col))],
                    ag_recv.at[i, j - 1], ag_send.at[i, j - 1])

    for g in range(groups):
        vec[0, g] = rhs_ref[:, g * LANES:(g + 1) * LANES]
    split_into(near_x, vec.at[0])
    products[slots] = jnp.zeros((series, tile), jnp.float32)
    pl.semaphore_wait(barrier, n_row - 1 + n_col - 1)

    for i in range(ITERS):
        far_start(i)
        if i == 1:
            exchange_start(0, [dot(lambda g: vec[0, g], lambda g: vec[0, g]),
                               dot(lambda g: vec[0, g], lambda g: vec[1, g])])
            split_into(near_x, vec.at[1])
        else:
            fetch.wait()
        multiply(rows_ref, near_x, 0)
        collect(mirror.at[i], False)
        mirror_start(i)
        far_relay(i)
        mirror_relay(i)
        far_done(i)
        multiply(cols_ref, far_x, 1)
        collect(direct.at[i], True)
        mirror_done(i)
        reduce_start(i)
        if i == 1:
            norm_now, curvature = exchange_done(0, 2)
            alpha0 = norm_now / curvature
            def leave(g, total):
                left = vec[0, g] - alpha0 * vec[1, g]
                r_one[g] = left
                return total + left * left
            partial = lax.fori_loop(0, groups, leave, jnp.zeros((series, LANES), jnp.float32))
            exchange_start(1, [partial])
        reduce_done(i)
        gather_start(i)
        if i == 1:
            (norm_next,) = exchange_done(1, 1)
            beta0 = norm_next / norm_now
            def turn(g, carry):
                p_one[g] = r_one[g] + beta0 * vec[0, g]
                return carry
            lax.fori_loop(0, groups, turn, 0)
        gather_done(i)

    def image(g):
        return vec[1, g] + beta0 * vec[1, g] - alpha0 * vec[2, g]
    exchange_start(2, [dot(image, lambda g: p_one[g])])
    (curvature1,) = exchange_done(2, 1)
    alpha1 = norm_next / curvature1
    for g in range(groups):
        lanes = slice(g * LANES, (g + 1) * LANES)
        solution_ref[:, lanes] = alpha0 * vec[0, g] + alpha1 * p_one[g]
        residual_ref[:, lanes] = r_one[g] - alpha1 * image(g)
    for wait in finals:
        wait()


def on_device(n_row, n_col, right_sides, nugget, cov_blocks, block_rows, block_cols, block_count):
    slots, tile = cov_blocks.shape[2:4]
    series, width = right_sides.shape
    tiles = width // tile
    groups = width // LANES
    chunk = groups // n_col
    chips = n_row // CORES
    rows, cols = block_rows[0, 0], block_cols[0, 0]
    slot_ids = jnp.arange(slots, dtype=jnp.int32)
    cell = jnp.where(slot_ids < block_count[0, 0], rows * tiles + cols, -1)
    cells = jnp.arange(tiles * tiles, dtype=jnp.int32)
    found = jnp.where(cell[None, :] == cells[:, None], slots - slot_ids[None, :], 0)
    pos = slots - jnp.max(found, axis=1)

    f32 = jnp.float32
    field = (groups, series, LANES)
    half = (groups, series // CORES, LANES)
    dma = pltpu.SemaphoreType.DMA
    smem = pl.BlockSpec(memory_space=pltpu.SMEM)
    vmem = pl.BlockSpec(memory_space=pltpu.VMEM)
    return pl.pallas_call(
        functools.partial(kernel, n_row, n_col),
        out_shape=(jax.ShapeDtypeStruct((series, width), f32),) * 2,
        in_specs=[smem, smem, smem, vmem, vmem, pl.BlockSpec(memory_space=pl.ANY)],
        out_specs=(vmem, vmem),
        scratch_shapes=[
            pltpu.VMEM((slots, tile, tile), jnp.bfloat16),
            pltpu.VMEM((ITERS + 1,) + field, f32),
            pltpu.VMEM((ITERS,) + field, f32),
            pltpu.VMEM((tiles, PIECES * series, tile), jnp.bfloat16),
            pltpu.VMEM((tiles, PIECES * series, tile), jnp.bfloat16),
            pltpu.VMEM((slots + 1, series, tile), f32),
            pltpu.VMEM((ITERS,) + field, f32),
            pltpu.VMEM((ITERS,) + field, f32),
            pltpu.VMEM((ITERS,) + half, f32),
            pltpu.VMEM((ITERS,) + half, f32),
            pltpu.VMEM((ITERS, chips) + field, f32),
            pltpu.VMEM((ITERS, n_col - 1, chunk, series, LANES), f32),
            pltpu.VMEM(field, f32),
            pltpu.VMEM(field, f32),
            pltpu.VMEM((3, 2, series, LANES), f32),
            pltpu.VMEM((3, n_row - 1, 2, series, LANES), f32),
            dma,
            dma((ITERS, chips, CORES)), dma((ITERS, CORES)), dma((ITERS,)),
            dma((ITERS,)), dma((ITERS,)), dma((ITERS,)), dma((ITERS, chips, CORES)),
            dma((ITERS, n_col - 1)), dma((ITERS, n_col - 1)),
            dma((ITERS, n_col - 1)), dma((ITERS, n_col - 1)),
            dma((3, n_row - 1)), dma((3, n_row - 1)),
        ],
        compiler_params=pltpu.CompilerParams(collective_id=0, has_side_effects=True),
    )(cols, rows, pos, right_sides, nugget.reshape(groups, LANES), cov_blocks[0, 0])


def solution(mesh):
    placed = (
        P(None, ("groups", "row")),
        P(("groups", "row")),
        P(("groups", "row"), "col", None, None, None),
        P(("groups", "row"), "col", None),
        P(("groups", "row"), "col", None),
        P(("groups", "row"), "col"),
    )
    return jax.shard_map(
        functools.partial(on_device, mesh.shape["row"], mesh.shape["col"]),
        mesh=mesh,
        in_specs=placed,
        out_specs=(P(None, ("groups", "row")), P(None, ("groups", "row"))),
        check_vma=False,
    )
```

time: 211 us -> 58.3 us (0.28)
  waiting for transfers between devices: 141 us -> 0 us
  Pallas kernels: 0 us -> 52.2 us
  matrix products: 25.7 us -> 0 us
  between operations: 14.7 us -> 1.29 us
  blocking collectives: 11.3 us -> 0 us
  other arithmetic: 9.03 us -> 1.29 us
  local copies, waits for them, and re-layouts: 8.58 us -> 3.34 us
    psum x4 -> x0, waiting for transfers between devices: 141 us -> none  [the longest x2 71.7 us: on_device(): total = lax.psum(apply_direct, 'col')]
    pallas_call x0 -> x1, Pallas kernels: none -> 52.2 us  [on_device(): pl.pallas_call(functools.partial(kernel, n_row, n_col), out_shape=(jax.Sh...]
    dot_general x8 -> x0, matrix products: 25.7 us -> none  [the longest x2 12 us: on_device(): jnp.einsum('rmk,mjk->rmj', jnp.take(far_tiles, slot_cols, axis=1), blocks...]
    psum x2 -> x0, blocking collectives: 11.3 us -> none  [on_device(): lax.psum((jnp.sum(direction * applied, axis=1), jnp.sum(residual * applie...]
    gather x4 -> x0, local copies, waits for them, and re-layouts: 4.37 us -> none  [the longest x2 3.14 us: on_device(): jnp.take(far_tiles, slot_cols, axis=1)]
    reshape x4 -> x0, local copies, waits for them, and re-layouts: 2.44 us -> none  [the longest x2 1.45 us: on_device(): far_tiles = far_rows.reshape(series, tile_count, tile_size)]
    reduce_sum x2 -> x0, other arithmetic: 2.25 us -> none  [on_device(): jnp.sum(direction * applied, axis=1)]
  transfers between devices with their start and end apart: 4 -> 0, of which waited for: 4 -> 0; matrix products, arithmetic and copies ran while one was open for 0% -> 0% of each run, Pallas kernels for 0% -> 0%
where the time goes in v1:
time: 58.3 us; the launch traced here: 58.1 us
  Pallas kernels  52.2 us (90%)
  local copies, waits for them, and re-layouts  3.34 us (6%)
  other arithmetic  1.29 us (2%)
  between operations  1.29 us (2%)
    pallas_call x1, Pallas kernels, on_device(): pl.pallas_call(functools.partial(kernel, n_row, n_col), out_shape=(jax.Sh...  52.2 us
    unnamed x2, local copies, waits for them, and re-layouts  3.34 us

profile of v1, /device:TPU:0, one launch (start us, length us, event | category | flops | bytes accessed | tf_op | source)
XLA Modules:
  0.0 58.1 jit_solution(3552514821089136154)
XLA Ops:
  1.3 0.7 %compare_select_fusion = (s32[32]{0:T(128)S(1)}, s32[32]{0:T(128)S(1)}) fusion(s32[]{:T(128)} %bitcast.7, s32[1,1,32]{2,1,0:T(1,128)} %param.9, s32[1,1,32]{2,1,0:T(1,128)} %param.10), kind=kLoop, calls=%fused_computation.2 | loop fusion | flops 160 | bytes 516 | tf_op jit(solution)/shard_map/jit(_where)/select_n | solution.py:304
  2.0 0.1 select_reduce_fusion
  2.0 0.5 broadcast_subtract_fusion.pos_ref
  2.6 52.2 %shard_map.77 = (f32[32,2048]{1,0:T(8,128)}, f32[32,2048]{1,0:T(8,128)}) custom-call(s32[32]{0:T(128)} %bitcast.10, s32[32]{0:T(128)} %bitcast.11, s32[64]{0:T(128)} %broadcast_subtract_fusion.pos_ref, f32[32,2048]{1,0:T(8,128)} %rhs_ref.1, f32[16,128]{1,0:T(8,128)} %bitcast.9, bf16[32,256,256]{2,1,0:T(8,128)(2,1)} %bitcast.8), custom_call_target="tpu_custom_call" | custom-call | tf_op jit(solution)/shard_map/pallas_call | solution.py:315
  54.7 1.7 %copy.11 = f32[32,2048]{1,0:T(8,128)} copy(f32[32,2048]{1,0:T(8,128)} %get-tuple-element.6) | data formatting | bytes 524288
  56.4 1.7 %copy.12 = f32[32,2048]{1,0:T(8,128)} copy(f32[32,2048]{1,0:T(8,128)} %get-tuple-element.7) | data formatting | bytes 524288

commit v2 on v1

v2 whole, which is shorter than its diff:
```python
import functools

import jax
import jax.numpy as jnp
from jax import lax
from jax.experimental import pallas as pl
from jax.experimental.pallas import tpu as pltpu
from jax.sharding import PartitionSpec as P

ITERS = 2
LANES = 128
CORES = 2
PIECES = 3
UNROLL = 8
BATCHES = 2


def kernel(
    n_row, n_col,
    cols_ref, rows_ref, pos_ref, rhs_ref, nugget_ref, stored_ref,
    start_ref, p_ref, r_ref, image_ref, step_ref,
    blocks, turned, vec, far, near_x, far_x, products, direct, mirror,
    m_part, m_half, m_root, rs_in, r_one, p_one, ex_out, ex_in,
    block_sem, far_send, far_recv, fwd_send, mp_send, mp_recv, mr_send, mr_recv,
    rs_send, rs_recv, ag_send, ag_recv, ex_send, ex_recv,
):
    batches, groups, series, _ = vec.shape[1:]
    slots, tile, _ = blocks.shape
    tiles = near_x.shape[1]
    per_tile = tile // LANES
    chunk = groups // n_col
    chips = n_row // CORES
    half_groups = groups // CORES
    me_row = lax.axis_index("row")
    me_col = lax.axis_index("col")
    chip, core = me_row // CORES, lax.rem(me_row, CORES)
    partner = chip * CORES + (1 - core)
    root = me_col
    root_chip = root // CORES
    is_root = me_row == root
    on_root_chip = chip == root_chip
    is_root_partner = jnp.logical_and(on_root_chip, jnp.logical_not(is_root))
    away = jnp.logical_not(on_root_chip)
    finals = []

    def copy(src, dst, send_sem, recv_sem, **where):
        return pltpu.make_async_remote_copy(
            src_ref=src, dst_ref=dst, send_sem=send_sem, recv_sem=recv_sem,
            device_id=where, device_id_type=pl.DeviceIdType.MESH)

    def arrived(dst, recv_sem, send_sem):
        copy(dst, dst, send_sem, recv_sem, row=partner).wait_recv()

    def own_half(ref, which):
        return ref.at[pl.ds(which * half_groups, half_groups)]

    def part(k):
        return pl.ds(k * chunk, chunk)

    barrier = pltpu.get_barrier_semaphore()
    for j in range(1, n_row):
        pl.semaphore_signal(barrier, inc=1, device_id={"row": lax.rem(me_row + j, n_row)},
                            device_id_type=pl.DeviceIdType.MESH)
    for j in range(1, n_col):
        pl.semaphore_signal(barrier, inc=1, device_id={"col": lax.rem(me_col + j, n_col)},
                            device_id_type=pl.DeviceIdType.MESH)
    fetch = pltpu.make_async_copy(stored_ref, blocks, block_sem)
    fetch.start()

    def split_into(dst, src):
        def one(t, carry):
            rest = jnp.concatenate([src[t * per_tile + k] for k in range(per_tile)], axis=1)
            tops = []
            for piece in range(PIECES):
                tops.append(rest.astype(jnp.bfloat16).astype(jnp.float32))
                rest = rest - tops[-1]
            dst[t] = jnp.concatenate(tops, axis=0).astype(jnp.bfloat16)
            return carry
        lax.fori_loop(0, tiles, one, 0)

    def multiply(pick_ref, x_ref, matrices):
        def some(step, carry):
            for k in range(UNROLL):
                s = step * UNROLL + k
                out = jnp.dot(x_ref[pick_ref[s]], matrices[s], preferred_element_type=jnp.float32)
                total = out[(PIECES - 1) * series:]
                for piece in range(PIECES - 2, -1, -1):
                    total = total + out[piece * series:(piece + 1) * series]
                products[s] = total
            return carry
        lax.fori_loop(0, slots // UNROLL, some, 0)

    def collect(dst, by_row):
        def one(t, carry):
            total = None
            for k in range(tiles):
                term = products[pos_ref[t * tiles + k] if by_row else pos_ref[k * tiles + t]]
                total = term if total is None else total + term
            for k in range(per_tile):
                dst[t * per_tile + k] = total[:, k * LANES:(k + 1) * LANES]
            return carry
        lax.fori_loop(0, tiles, one, 0)

    def dot(left, right):
        def one(g, total):
            return total + left(g) * right(g)
        return lax.fori_loop(0, groups, one, jnp.zeros((series, LANES), jnp.float32), unroll=4)

    def used(k):
        return pl.ds(0, 2 if k == 0 else 1)

    def exchange_start(k):
        for j in range(1, n_row):
            c = copy(ex_out.at[k, used(k)], ex_in.at[k, j - 1, used(k)], ex_send.at[k, j - 1], ex_recv.at[k, j - 1],
                     row=lax.rem(me_row + j, n_row))
            c.start()
            finals.append(c.wait_send)

    def exchange_done(k):
        for j in range(1, n_row):
            arrived(ex_in.at[k, j - 1, used(k)], ex_recv.at[k, j - 1], ex_send.at[k, j - 1])

    def exchanged(k, q, b):
        total = ex_out[k, q, b]
        for j in range(1, n_row):
            total = total + ex_in[k, j - 1, q, b]
        return jnp.sum(total, axis=1, keepdims=True)

    def far_start(i, b):
        for j in range(1, chips):
            for h in range(CORES):
                c = copy(own_half(vec.at[i, b], h), own_half(far.at[i, b], h),
                         far_send.at[i, b, j, h], far_recv.at[i, b, h],
                         row=lax.rem(root_chip + j, chips) * CORES + h)
                pl.when(is_root)(c.start)
                finals.append(lambda c=c: pl.when(is_root)(c.wait_send))
        for h in range(CORES):
            c = copy(own_half(vec.at[i, b], h), own_half(far.at[i, b], h),
                     far_send.at[i, b, 0, h], far_recv.at[i, b, h], row=partner)
            pl.when(is_root)(c.start)
            finals.append(lambda c=c: pl.when(is_root)(c.wait_send))

    def far_relay(i, b):
        def go():
            mine = own_half(far.at[i, b], core)
            arrived(mine, far_recv.at[i, b, core], fwd_send.at[i, b])
            copy(mine, mine, fwd_send.at[i, b], far_recv.at[i, b, core], row=partner).start()
        pl.when(away)(go)
        mine = own_half(far.at[i, b], core)
        c = copy(mine, mine, fwd_send.at[i, b], far_recv.at[i, b, core], row=partner)
        finals.append(lambda: pl.when(away)(c.wait_send))

    def far_done(i, b):
        def last():
            arrived(own_half(far.at[i, b], 1 - core), far_recv.at[i, b, 1 - core], fwd_send.at[i, b])
        def both():
            for h in range(CORES):
                arrived(own_half(far.at[i, b], h), far_recv.at[i, b, h], fwd_send.at[i, b])
        pl.when(away)(last)
        pl.when(is_root_partner)(both)
        pl.when(is_root)(lambda: split_into(far_x.at[b], vec.at[i, b]))
        pl.when(jnp.logical_not(is_root))(lambda: split_into(far_x.at[b], far.at[i, b]))

    def mirror_start(i, b):
        other = copy(own_half(mirror.at[i, b], 1 - core), m_part.at[i, b], mp_send.at[i, b], mp_recv.at[i, b], row=partner)
        whole = copy(mirror.at[i, b], m_root.at[i, b, chips - 1], mp_send.at[i, b],
                     mr_recv.at[i, b, chips - 1, 0], row=root)
        pl.when(away)(other.start)
        pl.when(is_root_partner)(whole.start)
        finals.append(lambda: pl.when(away)(other.wait_send))
        finals.append(lambda: pl.when(is_root_partner)(whole.wait_send))

    def mirror_relay(i, b):
        slot = lax.rem(chip - root_chip + chips, chips) - 1
        slot = jnp.maximum(slot, 0)
        onward = copy(m_half.at[i, b], own_half(m_root.at[i, b, slot], core), mr_send.at[i, b],
                      mr_recv.at[i, b, slot, core], row=root)
        def go():
            arrived(m_part.at[i, b], mp_recv.at[i, b], mp_send.at[i, b])
            first = core * half_groups
            def one(g, carry):
                m_half[i, b, g] = mirror[i, b, first + g] + m_part[i, b, g]
                return carry
            lax.fori_loop(0, half_groups, one, 0, unroll=4)
            onward.start()
        pl.when(away)(go)
        finals.append(lambda: pl.when(away)(onward.wait_send))

    def mirror_done(i, b):
        def go():
            for j in range(chips - 1):
                for h in range(CORES):
                    arrived(own_half(m_root.at[i, b, j], h), mr_recv.at[i, b, j, h], mr_send.at[i, b])
            arrived(m_root.at[i, b, chips - 1], mr_recv.at[i, b, chips - 1, 0], mr_send.at[i, b])
            def one(g, carry):
                total = direct[i, b, g] + mirror[i, b, g]
                for j in range(chips):
                    total = total + m_root[i, b, j, g]
                direct[i, b, g] = total
                return carry
            lax.fori_loop(0, groups, one, 0, unroll=2)
        pl.when(is_root)(go)

    def reduce_start(i, b):
        for j in range(n_col - 1, 0, -1):
            to = lax.rem(me_col + j, n_col)
            c = copy(direct.at[i, b, part(to)], rs_in.at[i, b, j - 1], rs_send.at[i, b, j - 1],
                     rs_recv.at[i, b, j - 1], col=to)
            c.start()
            finals.append(c.wait_send)

    def reduce_done(i, b):
        for j in range(1, n_col):
            arrived(rs_in.at[i, b, j - 1], rs_recv.at[i, b, j - 1], rs_send.at[i, b, j - 1])
        for k in range(chunk):
            g = me_col * chunk + k
            total = direct[i, b, g] + nugget_ref[pl.ds(g, 1), :] * vec[i, b, g]
            for j in range(1, n_col):
                total = total + rs_in[i, b, j - 1, k]
            vec[i + 1, b, g] = total

    def gather_start(i, b):
        mine = vec.at[i + 1, b, part(me_col)]
        for j in range(n_col - 1, 0, -1):
            c = copy(mine, mine, ag_send.at[i, b, j - 1], ag_recv.at[i, b, j - 1],
                     col=lax.rem(me_col + j, n_col))
            c.start()
            finals.append(c.wait_send)

    def gather_done(i, b):
        for j in range(1, n_col):
            arrived(vec.at[i + 1, b, part(lax.rem(me_col - j + n_col, n_col))],
                    ag_recv.at[i, b, j - 1], ag_send.at[i, b, j - 1])

    for b in range(batches):
        rows = slice(b * series, (b + 1) * series)
        for g in range(groups):
            vec[0, b, g] = rhs_ref[rows, g * LANES:(g + 1) * LANES]
    pl.semaphore_wait(barrier, n_row - 1 + n_col - 1)
    for b in range(batches):
        far_start(0, b)
    products[slots] = jnp.zeros((series, tile), jnp.float32)

    def mirror_part(i, b):
        split_into(near_x.at[b], vec.at[i, b])
        if i == 0 and b == 0:
            fetch.wait()
        multiply(rows_ref, near_x.at[b], blocks)
        collect(mirror.at[i, b], False)

    def relay_part(i, b):
        mirror_relay(i, b)
        far_relay(i, b)

    def direct_part(i, b):
        far_done(i, b)
        multiply(cols_ref, far_x.at[b], turned)
        collect(direct.at[i, b], True)
        mirror_done(i, b)
        reduce_start(i, b)

    def middle(i):
        relay_part(i, 0)
        for b in range(batches):
            if b + 1 < batches:
                relay_part(i, b + 1)
            if i == 0 and b == 0:
                lax.fori_loop(slots // 2, slots, transpose, 0, unroll=4)
            direct_part(i, b)

    for b in range(batches):
        mirror_part(0, b)
    for b in range(batches):
        mirror_start(0, b)
    def transpose(s, carry):
        turned[s] = blocks[s].T
        return carry
    lax.fori_loop(0, slots // 2, transpose, 0, unroll=4)
    middle(0)
    for b in range(batches):
        reduce_done(0, b)
        gather_start(0, b)
    for b in range(batches):
        ex_out[0, 0, b] = dot(lambda g: vec[0, b, g], lambda g: vec[0, b, g])
    for b in range(batches):
        gather_done(0, b)
        far_start(1, b)
        mirror_part(1, b)
        mirror_start(1, b)
        ex_out[0, 1, b] = dot(lambda g: vec[0, b, g], lambda g: vec[1, b, g])
    exchange_start(0)
    middle(1)
    exchange_done(0)
    norm_now = [exchanged(0, 0, b) for b in range(batches)]
    alpha0 = [norm_now[b] / exchanged(0, 1, b) for b in range(batches)]
    for b in range(batches):
        def leave(g, total):
            left = vec[0, b, g] - alpha0[b] * vec[1, b, g]
            r_one[b, g] = left
            return total + left * left
        ex_out[1, 0, b] = lax.fori_loop(0, groups, leave, jnp.zeros((series, LANES), jnp.float32))
    exchange_start(1)
    for b in range(batches):
        reduce_done(1, b)
        gather_start(1, b)
    exchange_done(1)
    norm_next = [exchanged(1, 0, b) for b in range(batches)]
    beta0 = [norm_next[b] / norm_now[b] for b in range(batches)]
    for b in range(batches):
        def turn(g, carry):
            p_one[b, g] = r_one[b, g] + beta0[b] * vec[0, b, g]
            return carry
        lax.fori_loop(0, groups, turn, 0)

    def image(b, g):
        return vec[1, b, g] + beta0[b] * vec[1, b, g] - alpha0[b] * vec[2, b, g]
    for b in range(batches):
        gather_done(1, b)
        ex_out[2, 0, b] = dot(lambda g: image(b, g), lambda g: p_one[b, g])
    exchange_start(2)
    for b in range(batches):
        rows = slice(b * series, (b + 1) * series)
        for g in range(groups):
            lanes = slice(g * LANES, (g + 1) * LANES)
            start_ref[rows, lanes] = alpha0[b] * vec[0, b, g]
            p_ref[rows, lanes] = p_one[b, g]
            r_ref[rows, lanes] = r_one[b, g]
            image_ref[rows, lanes] = image(b, g)
    exchange_done(2)
    for b in range(batches):
        rows = slice(b * series, (b + 1) * series)
        alpha1 = norm_next[b] / exchanged(2, 0, b)
        step_ref[rows, :] = jnp.broadcast_to(alpha1, (series, groups * LANES))
    for wait in finals:
        wait()


def on_device(n_row, n_col, right_sides, nugget, cov_blocks, block_rows, block_cols, block_count):
    slots, tile = cov_blocks.shape[2:4]
    series, width = right_sides.shape
    tiles = width // tile
    groups = width // LANES
    chunk = groups // n_col
    chips = n_row // CORES
    rows, cols = block_rows[0, 0], block_cols[0, 0]
    slot_ids = jnp.arange(slots, dtype=jnp.int32)
    cells = jnp.arange(tiles * tiles, dtype=jnp.int32)[:, None]
    live = slot_ids[None, :] < block_count
    here = jnp.logical_and(rows[None, :] * tiles + cols[None, :] == cells, live)
    pos = jnp.min(jnp.where(here, slot_ids[None, :], slots), axis=1)

    f32 = jnp.float32
    batch = series // BATCHES
    runs = (ITERS, BATCHES)
    field = (groups, batch, LANES)
    half = (groups // CORES, batch, LANES)
    dma = pltpu.SemaphoreType.DMA
    smem = pl.BlockSpec(memory_space=pltpu.SMEM)
    vmem = pl.BlockSpec(memory_space=pltpu.VMEM)
    start, turn, left, image, step = pl.pallas_call(
        functools.partial(kernel, n_row, n_col),
        out_shape=(jax.ShapeDtypeStruct((series, width), f32),) * 5,
        in_specs=[smem, smem, smem, vmem, vmem, pl.BlockSpec(memory_space=pl.ANY)],
        out_specs=(vmem,) * 5,
        scratch_shapes=[
            pltpu.VMEM((slots, tile, tile), jnp.bfloat16),
            pltpu.VMEM((slots, tile, tile), jnp.bfloat16),
            pltpu.VMEM((ITERS + 1, BATCHES) + field, f32),
            pltpu.VMEM(runs + field, f32),
            pltpu.VMEM((BATCHES, tiles, PIECES * batch, tile), jnp.bfloat16),
            pltpu.VMEM((BATCHES, tiles, PIECES * batch, tile), jnp.bfloat16),
            pltpu.VMEM((slots + 1, batch, tile), f32),
            pltpu.VMEM(runs + field, f32),
            pltpu.VMEM(runs + field, f32),
            pltpu.VMEM(runs + half, f32),
            pltpu.VMEM(runs + half, f32),
            pltpu.VMEM(runs + (chips,) + field, f32),
            pltpu.VMEM(runs + (n_col - 1, chunk, batch, LANES), f32),
            pltpu.VMEM((BATCHES,) + field, f32),
            pltpu.VMEM((BATCHES,) + field, f32),
            pltpu.VMEM((3, 2, BATCHES, batch, LANES), f32),
            pltpu.VMEM((3, n_row - 1, 2, BATCHES, batch, LANES), f32),
            dma,
            dma(runs + (chips, CORES)), dma(runs + (CORES,)), dma(runs),
            dma(runs), dma(runs), dma(runs), dma(runs + (chips, CORES)),
            dma(runs + (n_col - 1,)), dma(runs + (n_col - 1,)),
            dma(runs + (n_col - 1,)), dma(runs + (n_col - 1,)),
            dma((3, n_row - 1)), dma((3, n_row - 1)),
        ],
        compiler_params=pltpu.CompilerParams(collective_id=0, has_side_effects=True),
    )(cols, rows, pos, right_sides, nugget.reshape(groups, LANES), cov_blocks[0, 0])
    return start + step * turn, left - step * image


def solution(mesh):
    placed = (
        P(None, ("groups", "row")),
        P(("groups", "row")),
        P(("groups", "row"), "col", None, None, None),
        P(("groups", "row"), "col", None),
        P(("groups", "row"), "col", None),
        P(("groups", "row"), "col"),
    )
    return jax.shard_map(
        functools.partial(on_device, mesh.shape["row"], mesh.shape["col"]),
        mesh=mesh,
        in_specs=placed,
        out_specs=(P(None, ("groups", "row")), P(None, ("groups", "row"))),
        check_vma=False,
    )
```

time: 58.3 us -> 54.1 us (0.928)
  local copies, waits for them, and re-layouts: 3.34 us -> 0 us
  Pallas kernels: 52.2 us -> 49.2 us
  other arithmetic: 1.29 us -> 3.42 us
    unnamed x2 -> x0, local copies, waits for them, and re-layouts: 3.34 us -> none
    pallas_call x1, Pallas kernels: 52.2 us -> 49.2 us  [on_device(): pl.pallas_call(functools.partial(kernel, n_row, n_col), out_shape=(jax.Sh...]
    sub x1, other arithmetic: 0.52 us -> 2.13 us  [on_device(): return (start + step * turn, left - step * image)]
    select_n x1 -> x0, other arithmetic: 0.68 us -> none  [on_device(): cell = jnp.where(slot_ids < block_count[0, 0], rows * tiles + cols, -1)]
    add x0 -> x1, other arithmetic: none -> 0.68 us  [on_device(): here = jnp.logical_and(rows[None, :] * tiles + cols[None, :] == cells, live)]
    reduce_min x0 -> x1, other arithmetic: none -> 0.61 us  [on_device(): pos = jnp.min(jnp.where(here, slot_ids[None, :], slots), axis=1)]
where the time goes in v2:
time: 54.1 us; the launch traced here: 53.9 us
  Pallas kernels  49.2 us (91%)
  other arithmetic  3.42 us (6%)
  between operations  1.29 us (2%)
    pallas_call x1, Pallas kernels, on_device(): pl.pallas_call(functools.partial(kernel, n_row, n_col), out_shape=(jax.Sh...  49.2 us
    sub x1, other arithmetic, on_device(): return (start + step * turn, left - step * image)  2.13 us

profile of v2, /device:TPU:0, one launch (start us, length us, event | category | flops | bytes accessed | tf_op | source)
XLA Modules:
  0.0 53.9 jit_solution(5113881279698262462)
XLA Ops:
  1.3 0.7 %multiply_add_fusion.1 = s32[32]{0:T(128)S(1)} fusion(s32[1,1,32]{2,1,0:T(1,128)} %param.9, s32[1,1,32]{2,1,0:T(1,128)} %param.10), kind=kLoop, calls=%fused_computation.6 | loop fusion | flops 64 | bytes 384 | tf_op jit(solution)/shard_map/add | solution.py:349
  2.0 0.6 %select_reduce_fusion.pos_ref = s32[64]{0:T(128)} fusion(s32[32]{0:T(128)S(1)} %multiply_add_fusion.1, pred[32]{0:T(512)(128)(4,1)S(1)} %iota_compare_fusion.1), kind=kLoop, calls=%fused_computation.2 | loop fusion | flops 8128 | bytes 416 | tf_op jit(solution)/shard_map/reduce_min | solution.py:350
  2.6 49.2 %shard_map.77 = (f32[32,2048]{1,0:T(8,128)}, f32[32,2048]{1,0:T(8,128)}, f32[32,2048]{1,0:T(8,128)}, f32[32,2048]{1,0:T(8,128)}, f32[32,2048]{1,0:T(8,128)}) custom-call(s32[32]{0:T(128)} %bitcast.10, s32[32]{0:T(128)} %bitcast.11, s32[64]{0:T(128)} %select_reduce_fusion.pos_ref, f32[32,2048]{1,0:T(8,128)} %rhs_ref.1, f32[16,128]{1,0:T(8,128)} %bitcast.9, ...), custom_call_target="tpu_custom_call" | custom-call | tf_op jit(solution)/shard_map/pallas_call | solution.py:360
  51.8 2.1 %multiply_subtract_fusion = (f32[32,2048]{1,0:T(8,128)}, f32[32,2048]{1,0:T(8,128)}) fusion(f32[32,2048]{1,0:T(8,128)} %get-tuple-element.10, f32[32,2048]{1,0:T(8,128)} %get-tuple-element.8, f32[32,2048]{1,0:T(8,128)} %get-tuple-element.11, f32[32,2048]{1,0:T(8,128)} %get-tuple-element.7, f32[32,2048]{1,0:T(8,128)} %get-tuple-element.9), kind=kLoop, calls=%fused_computation | loop fusion | flops 262144 | bytes 1835008 | tf_op jit(solution)/shard_map/sub | solution.py:392
  (1 shorter events, 0.0 us)
